TPU v7x, 32 devices: a whole 2x2x4 slice. The times are simulated.
32 devices in a mesh: rep: 2 (over y), slab: 16 (over z, x, core).
Axes of the slice: x: 2, y: 2, z: 4, core: 2. Of those that a mesh axis runs over, the one named last changes fastest.
Arguments:
- spins: float32 [8, 3, 128, 16, 256], P('rep', None, 'slab'), as said below
- couplings: int32 [3, 128, 16, 256], P(None, 'slab'), may hold values from 0 to 1
- source: int32 [8], replicated, may hold values from 0 to 7, as said below
Outputs:
- annealed: float32 [8, 3, 128, 16, 256], P('rep', None, 'slab')
Inputs may be any that keep to these rules, and one draw needn't show every extreme that they name: Slot d = g * 4 + l (rep group g, local index l) either copies its own replica (source[d] = d) or copies a replica of group (g + 1 + l // 2) mod 2 whose own slot copies itself. In every group at least one of slots 0 and 1 and at least one of slots 2 and 3 copy in this way. Some group has two slots that copy replicas of one other group. `spins`: each replica is a unit vector at every site.
All inputs are finite; a program needn't handle non-finite values.
Results may differ from a plain program's by a relative error of at most 0.0003.
Values sent between devices are 32-bit elements; how exact they have to be, the bound alone decides.
A program may use at most 64 MiB of HBM per device.

v0:
```python
import jax
import jax.numpy as jnp
from jax import lax
from jax.sharding import PartitionSpec as P

SWEEPS = 4


def from_behind(value, axis, steps):
    count = lax.axis_size(axis)
    pairs = [(source, (source + steps) % count) for source in range(count)]
    return lax.ppermute(value, axis, pairs)


def with_halo(value, sides, width):
    for axis, dim in sides:
        devices, length = (lax.axis_size(axis), value.shape[dim])
        up = [(i, (i + 1) % devices) for i in range(devices)]
        down = [(j, i) for i, j in up]
        last = lax.slice_in_dim(value, length - width, length, axis=dim)
        leading = lax.slice_in_dim(value, 0, width, axis=dim)
        before = lax.ppermute(last, axis, up)
        after = lax.ppermute(leading, axis, down)
        value = jnp.concatenate([before, value, after], axis=dim)
    return value


def field(padded, bond_x, bond_y, bond_z):
    middle = padded[:, :, 1:-1]
    east = bond_x * jnp.roll(middle, -1, axis=4)
    west = jnp.roll(bond_x * middle, 1, axis=4)
    north = bond_y * jnp.roll(middle, -1, axis=3)
    south = jnp.roll(bond_y * middle, 1, axis=3)
    upper = bond_z[1:] * padded[:, :, 2:]
    lower = bond_z[:-1] * padded[:, :, :-2]
    return east + west + north + south + upper + lower


def relax(middle, local_field, mask):
    along = jnp.sum(middle * local_field, axis=1, keepdims=True)
    strength = jnp.sum(local_field * local_field, axis=1, keepdims=True)
    turned = 2.0 * along / jnp.maximum(strength, 1.0) * local_field - middle
    return jnp.where(mask, turned, middle)


def parity(planes, rows, cols, colour):
    shape = (planes, rows, cols)
    total = (
        lax.broadcasted_iota(jnp.int32, shape, 0)
        + lax.broadcasted_iota(jnp.int32, shape, 1)
        + lax.broadcasted_iota(jnp.int32, shape, 2)
    )
    return (total % 2 == colour)[None, None]


def local(spins, couplings, source):
    rep_dev = spins.shape[0]
    planes = spins.shape[2]
    rows = spins.shape[3]
    cols = spins.shape[4]
    group = lax.axis_index("rep")
    slots = group * rep_dev + jnp.arange(rep_dev, dtype=jnp.int32)
    wanted = jnp.take(source, slots)
    count = lax.axis_size("rep")

    def outgoing(offset):
        target = (group - offset) % count
        asked = jnp.take(
            source, target * rep_dev + 2 * (offset - 1) + jnp.arange(2, dtype=jnp.int32)
        )
        return jnp.take(spins, asked % rep_dev, axis=0)

    nearer = from_behind(outgoing(1), "rep", -1)
    farther = from_behind(outgoing(2), "rep", -2)
    arrived = jnp.concatenate([nearer, farther], axis=0)
    current = jnp.where((wanted == slots)[:, None, None, None, None], spins, arrived)
    bonds = (2 * couplings - 1).astype(jnp.float32)
    below = from_behind(couplings[2, planes - 1 :], "slab", 1)
    bond_z = jnp.concatenate([(2 * below - 1).astype(jnp.float32), bonds[2]], axis=0)
    masks = [parity(planes, rows, cols, colour) for colour in range(2)]
    for sweep in range(SWEEPS):
        for colour in range(2):
            padded = with_halo(current, (("slab", 2),), 1)
            local_field = field(padded, bonds[0], bonds[1], bond_z)
            current = relax(current, local_field, masks[colour])
    return current


def solution(mesh):
    in_specs = (P("rep", None, "slab", None, None), P(None, "slab", None, None), P())
    out_specs = P("rep", None, "slab", None, None)
    return jax.shard_map(local, mesh=mesh, in_specs=in_specs, out_specs=out_specs, check_vma=False)
```

profile of v0, /device:TPU:0, one launch (start us, length us, event | category | flops | bytes accessed | tf_op | source)
XLA Modules:
  0.0 129.2 jit_solution(5236444123382231078)
XLA Ops:
  2.5 2.1 %gather_fusion.4 = f32[2,3,8,16,256]{4,3,2,1,0:T(8,128)S(1)} fusion(f32[4,3,8,16,256]{4,3,2,1,0:T(8,128)} %param.7, s32[1024]{0:T(1024)S(1)} %pad_clamp_fusion), kind=kCustom, calls=%fused_computation.3.clone | custom fusion | bytes 1572872 | tf_op jit(solution)/shard_map/jit(_take)/gather | solution.py:71
  9.2 2.5 %collective-permute-start = (f32[2,3,8,16,256]{4,3,2,1,0:T(8,128)}, f32[2,3,8,16,256]{4,3,2,1,0:T(8,128)}, u32[]{:S(2)}, u32[]{:S(2)}) collective-permute-start(f32[2,3,8,16,256]{4,3,2,1,0:T(8,128)} %broadcast_select_fusion.1), channel_id=1, source_target_pairs={{0,16},{16,0},{1,17},{17,1},{2,18},{18,2},{3,19},{19,3},{4,20},{20... | collective-permute-start | bytes 2359304 | tf_op jit(solution)/shard_map/ppermute | solution.py:12
  13.4 16.0 %collective-permute-done = f32[2,3,8,16,256]{4,3,2,1,0:T(8,128)} collective-permute-done((f32[2,3,8,16,256]{4,3,2,1,0:T(8,128)}, f32[2,3,8,16,256]{4,3,2,1,0:T(8,128)}, u32[]{:S(2)}, u32[]{:S(2)}) %collective-permute-start) | collective-permute-done | bytes 786464 | tf_op jit(solution)/shard_map/ppermute | solution.py:12
  31.9 4.1 %collective-permute-start.2 = (f32[4,3,1,16,256]{4,3,2,1,0:T(8,128)S(1)}, f32[4,3,1,16,256]{4,3,2,1,0:T(8,128)S(1)}, u32[]{:S(2)}, u32[]{:S(2)}) collective-permute-start(f32[4,3,1,16,256]{4,3,2,1,0:T(8,128)S(1)} %get-tuple-element.65), channel_id=1, source_target_pairs={{1,0},{2,1},{3,2},{4,3},{5,4},{6,5},{7,6},{8,7},{9,8},{10,9},{11,1... | collective-permute-start | bytes 589832 | tf_op jit(solution)/shard_map/ppermute | solution.py:23
  36.5 2.7 %collective-permute-done.2 = f32[4,3,1,16,256]{4,3,2,1,0:T(8,128)S(1)} collective-permute-done((f32[4,3,1,16,256]{4,3,2,1,0:T(8,128)S(1)}, f32[4,3,1,16,256]{4,3,2,1,0:T(8,128)S(1)}, u32[]{:S(2)}, u32[]{:S(2)}) %collective-permute-start.2) | collective-permute-done | bytes 196640 | tf_op jit(solution)/shard_map/ppermute | solution.py:23
  39.2 4.6 %collective-permute-done.4 = f32[4,3,1,16,256]{4,3,2,1,0:T(8,128)S(1)} collective-permute-done((f32[4,3,1,16,256]{4,3,2,1,0:T(8,128)S(1)}, f32[4,3,1,16,256]{4,3,2,1,0:T(8,128)S(1)}, u32[]{:S(2)}, u32[]{:S(2)}) %collective-permute-start.4) | collective-permute-done | bytes 196640 | tf_op jit(solution)/shard_map/ppermute | solution.py:22
  43.8 2.0 %multiply_reduce_fusion.15 = (f32[4,8,16,256]{3,2,1,0:T(8,128)S(1)}, f32[4,8,16,256]{3,2,1,0:T(8,128)S(1)}, f32[4,3,8,16,256]{4,3,2,1,0:T(8,128)S(1)}) fusion(f32[4,3,8,16,256]{4,3,2,1,0:T(8,128)S(1)} %get-tuple-element.46, f32[4,3,1,16,256]{4,3,2,1,0:T(8,128)S(1)} %collective-permute-done.4, f32[8,16,256]{2,1,0:T(8,128)S(1)} %pad_maximum_fusion.16, ...), kind=kLoop, calls=%fused_computation.117 | loop fusion | flops 7208960 | bytes 11403264 | tf_op jit(solution)/shard_map/reduce_sum | solution.py:40
  48.6 2.3 %collective-permute-done.5 = f32[4,3,1,16,256]{4,3,2,1,0:T(8,128)S(1)} collective-permute-done((f32[4,3,1,16,256]{4,3,2,1,0:T(8,128)S(1)}, f32[4,3,1,16,256]{4,3,2,1,0:T(8,128)S(1)}, u32[]{:S(2)}, u32[]{:S(2)}) %collective-permute-start.5) | collective-permute-done | bytes 196640 | tf_op jit(solution)/shard_map/ppermute | solution.py:23
  50.9 4.6 %collective-permute-done.6 = f32[4,3,1,16,256]{4,3,2,1,0:T(8,128)S(1)} collective-permute-done((f32[4,3,1,16,256]{4,3,2,1,0:T(8,128)S(1)}, f32[4,3,1,16,256]{4,3,2,1,0:T(8,128)S(1)}, u32[]{:S(2)}, u32[]{:S(2)}) %collective-permute-start.6) | collective-permute-done | bytes 196640 | tf_op jit(solution)/shard_map/ppermute | solution.py:22
  55.5 2.0 %multiply_reduce_fusion.13 = (f32[4,8,16,256]{3,2,1,0:T(8,128)S(1)}, f32[4,8,16,256]{3,2,1,0:T(8,128)S(1)}, f32[4,3,8,16,256]{4,3,2,1,0:T(8,128)S(1)}) fusion(f32[4,3,8,16,256]{4,3,2,1,0:T(8,128)S(1)} %get-tuple-element.43, f32[4,3,1,16,256]{4,3,2,1,0:T(8,128)S(1)} %collective-permute-done.6, f32[8,16,256]{2,1,0:T(8,128)S(1)} %pad_maximum_fusion.16, ...), kind=kLoop, calls=%fused_computation.115 | loop fusion | flops 7208960 | bytes 11403264 | tf_op jit(solution)/shard_map/reduce_sum | solution.py:40
  60.2 2.3 %collective-permute-done.7 = f32[4,3,1,16,256]{4,3,2,1,0:T(8,128)S(1)} collective-permute-done((f32[4,3,1,16,256]{4,3,2,1,0:T(8,128)S(1)}, f32[4,3,1,16,256]{4,3,2,1,0:T(8,128)S(1)}, u32[]{:S(2)}, u32[]{:S(2)}) %collective-permute-start.7) | collective-permute-done | bytes 196640 | tf_op jit(solution)/shard_map/ppermute | solution.py:23
  62.5 4.6 %collective-permute-done.8 = f32[4,3,1,16,256]{4,3,2,1,0:T(8,128)S(1)} collective-permute-done((f32[4,3,1,16,256]{4,3,2,1,0:T(8,128)S(1)}, f32[4,3,1,16,256]{4,3,2,1,0:T(8,128)S(1)}, u32[]{:S(2)}, u32[]{:S(2)}) %collective-permute-start.8) | collective-permute-done | bytes 196640 | tf_op jit(solution)/shard_map/ppermute | solution.py:22
  67.2 2.0 %multiply_reduce_fusion.11 = (f32[4,8,16,256]{3,2,1,0:T(8,128)S(1)}, f32[4,8,16,256]{3,2,1,0:T(8,128)S(1)}, f32[4,3,8,16,256]{4,3,2,1,0:T(8,128)S(1)}) fusion(f32[4,3,8,16,256]{4,3,2,1,0:T(8,128)S(1)} %get-tuple-element.40, f32[4,3,1,16,256]{4,3,2,1,0:T(8,128)S(1)} %collective-permute-done.8, f32[8,16,256]{2,1,0:T(8,128)S(1)} %pad_maximum_fusion.16, ...), kind=kLoop, calls=%fused_computation.113 | loop fusion | flops 7208960 | bytes 11403264 | tf_op jit(solution)/shard_map/reduce_sum | solution.py:40
  71.9 2.2 %collective-permute-done.9 = f32[4,3,1,16,256]{4,3,2,1,0:T(8,128)S(1)} collective-permute-done((f32[4,3,1,16,256]{4,3,2,1,0:T(8,128)S(1)}, f32[4,3,1,16,256]{4,3,2,1,0:T(8,128)S(1)}, u32[]{:S(2)}, u32[]{:S(2)}) %collective-permute-start.9) | collective-permute-done | bytes 196640 | tf_op jit(solution)/shard_map/ppermute | solution.py:23
  74.1 4.8 %collective-permute-done.10 = f32[4,3,1,16,256]{4,3,2,1,0:T(8,128)S(1)} collective-permute-done((f32[4,3,1,16,256]{4,3,2,1,0:T(8,128)S(1)}, f32[4,3,1,16,256]{4,3,2,1,0:T(8,128)S(1)}, u32[]{:S(2)}, u32[]{:S(2)}) %collective-permute-start.10) | collective-permute-done | bytes 196640 | tf_op jit(solution)/shard_map/ppermute | solution.py:22
  79.0 2.0 %multiply_reduce_fusion.9 = (f32[4,8,16,256]{3,2,1,0:T(8,128)S(1)}, f32[4,8,16,256]{3,2,1,0:T(8,128)S(1)}, f32[4,3,8,16,256]{4,3,2,1,0:T(8,128)S(1)}) fusion(f32[4,3,8,16,256]{4,3,2,1,0:T(8,128)S(1)} %get-tuple-element.37, f32[4,3,1,16,256]{4,3,2,1,0:T(8,128)S(1)} %collective-permute-done.10, f32[8,16,256]{2,1,0:T(8,128)S(1)} %pad_maximum_fusion.16, ...), kind=kLoop, calls=%fused_computation.111 | loop fusion | flops 7208960 | bytes 11403264 | tf_op jit(solution)/shard_map/reduce_sum | solution.py:40
  83.7 2.2 %collective-permute-done.11 = f32[4,3,1,16,256]{4,3,2,1,0:T(8,128)S(1)} collective-permute-done((f32[4,3,1,16,256]{4,3,2,1,0:T(8,128)S(1)}, f32[4,3,1,16,256]{4,3,2,1,0:T(8,128)S(1)}, u32[]{:S(2)}, u32[]{:S(2)}) %collective-permute-start.11) | collective-permute-done | bytes 196640 | tf_op jit(solution)/shard_map/ppermute | solution.py:23
  85.9 4.7 %collective-permute-done.12 = f32[4,3,1,16,256]{4,3,2,1,0:T(8,128)S(1)} collective-permute-done((f32[4,3,1,16,256]{4,3,2,1,0:T(8,128)S(1)}, f32[4,3,1,16,256]{4,3,2,1,0:T(8,128)S(1)}, u32[]{:S(2)}, u32[]{:S(2)}) %collective-permute-start.12) | collective-permute-done | bytes 196640 | tf_op jit(solution)/shard_map/ppermute | solution.py:22
  95.3 2.2 %collective-permute-done.13 = f32[4,3,1,16,256]{4,3,2,1,0:T(8,128)S(1)} collective-permute-done((f32[4,3,1,16,256]{4,3,2,1,0:T(8,128)S(1)}, f32[4,3,1,16,256]{4,3,2,1,0:T(8,128)S(1)}, u32[]{:S(2)}, u32[]{:S(2)}) %collective-permute-start.13) | collective-permute-done | bytes 196640 | tf_op jit(solution)/shard_map/ppermute | solution.py:23
  97.5 4.7 %collective-permute-done.14 = f32[4,3,1,16,256]{4,3,2,1,0:T(8,128)S(1)} collective-permute-done((f32[4,3,1,16,256]{4,3,2,1,0:T(8,128)S(1)}, f32[4,3,1,16,256]{4,3,2,1,0:T(8,128)S(1)}, u32[]{:S(2)}, u32[]{:S(2)}) %collective-permute-start.14) | collective-permute-done | bytes 196640 | tf_op jit(solution)/shard_map/ppermute | solution.py:22
  106.9 2.2 %collective-permute-done.15 = f32[4,3,1,16,256]{4,3,2,1,0:T(8,128)S(1)} collective-permute-done((f32[4,3,1,16,256]{4,3,2,1,0:T(8,128)S(1)}, f32[4,3,1,16,256]{4,3,2,1,0:T(8,128)S(1)}, u32[]{:S(2)}, u32[]{:S(2)}) %collective-permute-start.15) | collective-permute-done | bytes 196640 | tf_op jit(solution)/shard_map/ppermute | solution.py:23
  109.2 4.7 %collective-permute-done.16 = f32[4,3,1,16,256]{4,3,2,1,0:T(8,128)S(1)} collective-permute-done((f32[4,3,1,16,256]{4,3,2,1,0:T(8,128)S(1)}, f32[4,3,1,16,256]{4,3,2,1,0:T(8,128)S(1)}, u32[]{:S(2)}, u32[]{:S(2)}) %collective-permute-start.16) | collective-permute-done | bytes 196640 | tf_op jit(solution)/shard_map/ppermute | solution.py:22
  118.6 2.2 %collective-permute-done.17 = f32[4,3,1,16,256]{4,3,2,1,0:T(8,128)S(1)} collective-permute-done((f32[4,3,1,16,256]{4,3,2,1,0:T(8,128)S(1)}, f32[4,3,1,16,256]{4,3,2,1,0:T(8,128)S(1)}, u32[]{:S(2)}, u32[]{:S(2)}) %collective-permute-start.17) | collective-permute-done | bytes 196640 | tf_op jit(solution)/shard_map/ppermute | solution.py:23
  120.8 4.7 %collective-permute-done.18 = f32[4,3,1,16,256]{4,3,2,1,0:T(8,128)S(1)} collective-permute-done((f32[4,3,1,16,256]{4,3,2,1,0:T(8,128)S(1)}, f32[4,3,1,16,256]{4,3,2,1,0:T(8,128)S(1)}, u32[]{:S(2)}, u32[]{:S(2)}) %collective-permute-start.18) | collective-permute-done | bytes 196640 | tf_op jit(solution)/shard_map/ppermute | solution.py:22
  (136 shorter events, 39.8 us)
Async XLA Ops:
  0.0 1.8 %copy-start = (s32[8]{0:T(128)S(1)}, s32[8]{0:T(128)}, u32[]{:S(2)}) copy-start(s32[8]{0:T(128)} %param.9) | copy-start | bytes 100
  1.3 11.3 %collective-permute-start.3 = (s32[1,16,256]{2,1,0:T(8,128)}, s32[1,16,256]{2,1,0:T(8,128)}, u32[]{:S(2)}, u32[]{:S(2)}) collective-permute-start(s32[1,16,256]{2,1,0:T(8,128)} %slice_bitcast_fusion.3), channel_id=1, source_target_pairs={{0,1},{1,2},{2,3},{3,4},{4,5},{5,6},{6,7},{7,8},{8,9},{9,10},{10,1... | collective-permute-start | bytes 49160 | tf_op jit(solution)/shard_map/ppermute | solution.py:12
  2.5 5.0 %copy-start.2 = (f32[4,3,8,16,256]{4,3,2,1,0:T(8,128)S(1)}, f32[4,3,8,16,256]{4,3,2,1,0:T(8,128)}, u32[]{:S(2)}) copy-start(f32[4,3,8,16,256]{4,3,2,1,0:T(8,128)} %param.7) | copy-start | bytes 4718596
  5.7 7.6 %collective-permute-start.1 = (f32[2,3,8,16,256]{4,3,2,1,0:T(8,128)}, f32[2,3,8,16,256]{4,3,2,1,0:T(8,128)S(1)}, u32[]{:S(2)}, u32[]{:S(2)}) collective-permute-start(f32[2,3,8,16,256]{4,3,2,1,0:T(8,128)} %broadcast_select_fusion), channel_id=1, source_target_pairs={{0,0},{16,16},{1,1},{17,17},{2,2},{18,18},{3,3},{19,19},{4,4},{20,... | collective-permute-start | bytes 2359304 | tf_op jit(solution)/shard_map/ppermute | solution.py:12
  7.5 4.2 %copy-start.3 = (s32[3,8,16,256]{3,2,1,0:T(8,128)S(1)}, s32[3,8,16,256]{3,2,1,0:T(8,128)}, u32[]{:S(2)}) copy-start(s32[3,8,16,256]{3,2,1,0:T(8,128)} %param.8) | copy-start | bytes 1179652
  9.2 20.1 %collective-permute-start = (f32[2,3,8,16,256]{4,3,2,1,0:T(8,128)}, f32[2,3,8,16,256]{4,3,2,1,0:T(8,128)}, u32[]{:S(2)}, u32[]{:S(2)}) collective-permute-start(f32[2,3,8,16,256]{4,3,2,1,0:T(8,128)} %broadcast_select_fusion.1), channel_id=1, source_target_pairs={{0,16},{16,0},{1,17},{17,1},{2,18},{18,2},{3,19},{19,3},{4,20},{20... | collective-permute-start | bytes 2359304 | tf_op jit(solution)/shard_map/ppermute | solution.py:12
  31.9 7.3 %collective-permute-start.2 = (f32[4,3,1,16,256]{4,3,2,1,0:T(8,128)S(1)}, f32[4,3,1,16,256]{4,3,2,1,0:T(8,128)S(1)}, u32[]{:S(2)}, u32[]{:S(2)}) collective-permute-start(f32[4,3,1,16,256]{4,3,2,1,0:T(8,128)S(1)} %get-tuple-element.65), channel_id=1, source_target_pairs={{1,0},{2,1},{3,2},{4,3},{5,4},{6,5},{7,6},{8,7},{9,8},{10,9},{11,1... | collective-permute-start | bytes 589832 | tf_op jit(solution)/shard_map/ppermute | solution.py:23
  36.0 7.8 %collective-permute-start.4 = (f32[4,3,1,16,256]{4,3,2,1,0:T(8,128)S(1)}, f32[4,3,1,16,256]{4,3,2,1,0:T(8,128)S(1)}, u32[]{:S(2)}, u32[]{:S(2)}) collective-permute-start(f32[4,3,1,16,256]{4,3,2,1,0:T(8,128)S(1)} %get-tuple-element.66), channel_id=1, source_target_pairs={{0,1},{1,2},{2,3},{3,4},{4,5},{5,6},{6,7},{7,8},{8,9},{9,10},{10,1... | collective-permute-start | bytes 589832 | tf_op jit(solution)/shard_map/ppermute | solution.py:22
  47.5 3.3 %collective-permute-start.5 = (f32[4,3,1,16,256]{4,3,2,1,0:T(8,128)S(1)}, f32[4,3,1,16,256]{4,3,2,1,0:T(8,128)S(1)}, u32[]{:S(2)}, u32[]{:S(2)}) collective-permute-start(f32[4,3,1,16,256]{4,3,2,1,0:T(8,128)S(1)} %get-tuple-element.63), channel_id=1, source_target_pairs={{1,0},{2,1},{3,2},{4,3},{5,4},{6,5},{7,6},{8,7},{9,8},{10,9},{11,1... | collective-permute-start | bytes 589832 | tf_op jit(solution)/shard_map/ppermute | solution.py:23
  47.7 7.8 %collective-permute-start.6 = (f32[4,3,1,16,256]{4,3,2,1,0:T(8,128)S(1)}, f32[4,3,1,16,256]{4,3,2,1,0:T(8,128)S(1)}, u32[]{:S(2)}, u32[]{:S(2)}) collective-permute-start(f32[4,3,1,16,256]{4,3,2,1,0:T(8,128)S(1)} %get-tuple-element.64), channel_id=1, source_target_pairs={{0,1},{1,2},{2,3},{3,4},{4,5},{5,6},{6,7},{7,8},{8,9},{9,10},{10,1... | collective-permute-start | bytes 589832 | tf_op jit(solution)/shard_map/ppermute | solution.py:22
  59.2 3.3 %collective-permute-start.7 = (f32[4,3,1,16,256]{4,3,2,1,0:T(8,128)S(1)}, f32[4,3,1,16,256]{4,3,2,1,0:T(8,128)S(1)}, u32[]{:S(2)}, u32[]{:S(2)}) collective-permute-start(f32[4,3,1,16,256]{4,3,2,1,0:T(8,128)S(1)} %get-tuple-element.61), channel_id=1, source_target_pairs={{1,0},{2,1},{3,2},{4,3},{5,4},{6,5},{7,6},{8,7},{9,8},{10,9},{11,1... | collective-permute-start | bytes 589832 | tf_op jit(solution)/shard_map/ppermute | solution.py:23
  59.4 7.8 %collective-permute-start.8 = (f32[4,3,1,16,256]{4,3,2,1,0:T(8,128)S(1)}, f32[4,3,1,16,256]{4,3,2,1,0:T(8,128)S(1)}, u32[]{:S(2)}, u32[]{:S(2)}) collective-permute-start(f32[4,3,1,16,256]{4,3,2,1,0:T(8,128)S(1)} %get-tuple-element.62), channel_id=1, source_target_pairs={{0,1},{1,2},{2,3},{3,4},{4,5},{5,6},{6,7},{7,8},{8,9},{9,10},{10,1... | collective-permute-start | bytes 589832 | tf_op jit(solution)/shard_map/ppermute | solution.py:22
  70.9 3.2 %collective-permute-start.9 = (f32[4,3,1,16,256]{4,3,2,1,0:T(8,128)S(1)}, f32[4,3,1,16,256]{4,3,2,1,0:T(8,128)S(1)}, u32[]{:S(2)}, u32[]{:S(2)}) collective-permute-start(f32[4,3,1,16,256]{4,3,2,1,0:T(8,128)S(1)} %get-tuple-element.59), channel_id=1, source_target_pairs={{1,0},{2,1},{3,2},{4,3},{5,4},{6,5},{7,6},{8,7},{9,8},{10,9},{11,1... | collective-permute-start | bytes 589832 | tf_op jit(solution)/shard_map/ppermute | solution.py:23
  70.9 8.0 %collective-permute-start.10 = (f32[4,3,1,16,256]{4,3,2,1,0:T(8,128)S(1)}, f32[4,3,1,16,256]{4,3,2,1,0:T(8,128)S(1)}, u32[]{:S(2)}, u32[]{:S(2)}) collective-permute-start(f32[4,3,1,16,256]{4,3,2,1,0:T(8,128)S(1)} %get-tuple-element.60), channel_id=1, source_target_pairs={{0,1},{1,2},{2,3},{3,4},{4,5},{5,6},{6,7},{7,8},{8,9},{9,10},{10,1... | collective-permute-start | bytes 589832 | tf_op jit(solution)/shard_map/ppermute | solution.py:22
  82.7 3.2 %collective-permute-start.11 = (f32[4,3,1,16,256]{4,3,2,1,0:T(8,128)S(1)}, f32[4,3,1,16,256]{4,3,2,1,0:T(8,128)S(1)}, u32[]{:S(2)}, u32[]{:S(2)}) collective-permute-start(f32[4,3,1,16,256]{4,3,2,1,0:T(8,128)S(1)} %get-tuple-element.57), channel_id=1, source_target_pairs={{1,0},{2,1},{3,2},{4,3},{5,4},{6,5},{7,6},{8,7},{9,8},{10,9},{11,1... | collective-permute-start | bytes 589832 | tf_op jit(solution)/shard_map/ppermute | solution.py:23
  82.7 7.8 %collective-permute-start.12 = (f32[4,3,1,16,256]{4,3,2,1,0:T(8,128)S(1)}, f32[4,3,1,16,256]{4,3,2,1,0:T(8,128)S(1)}, u32[]{:S(2)}, u32[]{:S(2)}) collective-permute-start(f32[4,3,1,16,256]{4,3,2,1,0:T(8,128)S(1)} %get-tuple-element.58), channel_id=1, source_target_pairs={{0,1},{1,2},{2,3},{3,4},{4,5},{5,6},{6,7},{7,8},{8,9},{9,10},{10,1... | collective-permute-start | bytes 589832 | tf_op jit(solution)/shard_map/ppermute | solution.py:22
  94.3 3.2 %collective-permute-start.13 = (f32[4,3,1,16,256]{4,3,2,1,0:T(8,128)S(1)}, f32[4,3,1,16,256]{4,3,2,1,0:T(8,128)S(1)}, u32[]{:S(2)}, u32[]{:S(2)}) collective-permute-start(f32[4,3,1,16,256]{4,3,2,1,0:T(8,128)S(1)} %get-tuple-element.55), channel_id=1, source_target_pairs={{1,0},{2,1},{3,2},{4,3},{5,4},{6,5},{7,6},{8,7},{9,8},{10,9},{11,1... | collective-permute-start | bytes 589832 | tf_op jit(solution)/shard_map/ppermute | solution.py:23
  94.4 7.8 %collective-permute-start.14 = (f32[4,3,1,16,256]{4,3,2,1,0:T(8,128)S(1)}, f32[4,3,1,16,256]{4,3,2,1,0:T(8,128)S(1)}, u32[]{:S(2)}, u32[]{:S(2)}) collective-permute-start(f32[4,3,1,16,256]{4,3,2,1,0:T(8,128)S(1)} %get-tuple-element.56), channel_id=1, source_target_pairs={{0,1},{1,2},{2,3},{3,4},{4,5},{5,6},{6,7},{7,8},{8,9},{9,10},{10,1... | collective-permute-start | bytes 589832 | tf_op jit(solution)/shard_map/ppermute | solution.py:22
  105.9 3.2 %collective-permute-start.15 = (f32[4,3,1,16,256]{4,3,2,1,0:T(8,128)S(1)}, f32[4,3,1,16,256]{4,3,2,1,0:T(8,128)S(1)}, u32[]{:S(2)}, u32[]{:S(2)}) collective-permute-start(f32[4,3,1,16,256]{4,3,2,1,0:T(8,128)S(1)} %get-tuple-element.53), channel_id=1, source_target_pairs={{1,0},{2,1},{3,2},{4,3},{5,4},{6,5},{7,6},{8,7},{9,8},{10,9},{11,1... | collective-permute-start | bytes 589832 | tf_op jit(solution)/shard_map/ppermute | solution.py:23
  106.0 7.8 %collective-permute-start.16 = (f32[4,3,1,16,256]{4,3,2,1,0:T(8,128)S(1)}, f32[4,3,1,16,256]{4,3,2,1,0:T(8,128)S(1)}, u32[]{:S(2)}, u32[]{:S(2)}) collective-permute-start(f32[4,3,1,16,256]{4,3,2,1,0:T(8,128)S(1)} %get-tuple-element.54), channel_id=1, source_target_pairs={{0,1},{1,2},{2,3},{3,4},{4,5},{5,6},{6,7},{7,8},{8,9},{9,10},{10,1... | collective-permute-start | bytes 589832 | tf_op jit(solution)/shard_map/ppermute | solution.py:22
  117.5 3.2 %collective-permute-start.17 = (f32[4,3,1,16,256]{4,3,2,1,0:T(8,128)S(1)}, f32[4,3,1,16,256]{4,3,2,1,0:T(8,128)S(1)}, u32[]{:S(2)}, u32[]{:S(2)}) collective-permute-start(f32[4,3,1,16,256]{4,3,2,1,0:T(8,128)S(1)} %get-tuple-element.51), channel_id=1, source_target_pairs={{1,0},{2,1},{3,2},{4,3},{5,4},{6,5},{7,6},{8,7},{9,8},{10,9},{11,1... | collective-permute-start | bytes 589832 | tf_op jit(solution)/shard_map/ppermute | solution.py:23
  117.6 7.8 %collective-permute-start.18 = (f32[4,3,1,16,256]{4,3,2,1,0:T(8,128)S(1)}, f32[4,3,1,16,256]{4,3,2,1,0:T(8,128)S(1)}, u32[]{:S(2)}, u32[]{:S(2)}) collective-permute-start(f32[4,3,1,16,256]{4,3,2,1,0:T(8,128)S(1)} %get-tuple-element.52), channel_id=1, source_target_pairs={{0,1},{1,2},{2,3},{3,4},{4,5},{5,6},{6,7},{7,8},{8,9},{9,10},{10,1... | collective-permute-start | bytes 589832 | tf_op jit(solution)/shard_map/ppermute | solution.py:22
  127.6 1.6 %copy-start.1 = (s32[8]{0:T(128)S(1)}, s32[8]{0:T(128)}, u32[]{:S(2)}) copy-start(s32[8]{0:T(128)} %param.9) | copy-start | bytes 100
where the time goes:
time: 130 us; the launch traced here: 129 us
  waiting for transfers between devices  71.8 us (55%)
  other arithmetic  28.9 us (22%)
  local copies, waits for them, and re-layouts  15.6 us (12%)
  starting transfers between devices  12.2 us (9%)
    ppermute x8, waiting for transfers between devices, with_halo(): before = lax.ppermute(last, axis, up)  37.3 us
    ppermute x8, waiting for transfers between devices, with_halo(): after = lax.ppermute(leading, axis, down)  18.5 us
    reduce_sum x8, other arithmetic, relax(): along = jnp.sum(middle * local_field, axis=1, keepdims=True)  16.2 us
    ppermute x3, waiting for transfers between devices, from_behind(): return lax.ppermute(value, axis, pairs)  16 us
    mul x8, other arithmetic, field(): south = jnp.roll(bond_y * middle, 1, axis=3)  5.79 us
    ppermute x8, starting transfers between devices, with_halo(): after = lax.ppermute(leading, axis, down)  4.73 us
    slice x16, local copies, waits for them, and re-layouts, field(): east = bond_x * jnp.roll(middle, -1, axis=4)  4.37 us
    ppermute x3, starting transfers between devices, from_behind(): return lax.ppermute(value, axis, pairs)  4.13 us
  transfers between devices with their start and end apart: 19, of which 17 were waited for; matrix products, arithmetic and copies ran while one was open for 9% of the time, Pallas kernels for 0%

commit v1 on v0

v1 whole, which is shorter than its diff:
```python
import functools

import jax
import jax.numpy as jnp
from jax import lax
from jax.experimental import pallas as pl
from jax.experimental.pallas import tpu as pltpu
from jax.sharding import PartitionSpec as P

SWEEPS = 4
WIDTH = 2
MESH = pl.DeviceIdType.MESH


def reverse_rows(value, row):
    count = value.shape[0]
    shift = 1
    while shift < count:
        down = pltpu.roll(value, shift, 0)
        if 2 * shift == count:
            value = down
        else:
            value = jnp.where((row & shift) == 0, pltpu.roll(value, count - shift, 0), down)
        shift *= 2
    return value


def halo_items(width, colour):
    below = [(0, 1 - colour)] + [(d, c) for d in range(1, width) for c in range(2)]
    above = [(d, c) for d in range(width - 1) for c in range(2)] + [(width - 1, 1 - colour)]
    return below, above


def kernel(n_rep, n_slab, source, spins, coup, out, work, bonds, low, high, stage, land, res, c_send, c_recv, h_send, h_recv, r_send, r_recv):
    rep_dev, comps, planes, rows, cols = spins.shape
    pairs = rep_dev // 2
    width, half = WIDTH, rows // 2
    exchanges = 2 * SWEEPS // width
    group, slab = lax.axis_index("rep"), lax.axis_index("slab")
    up, down = lax.rem(slab + 1, n_slab), lax.rem(slab + n_slab - 1, n_slab)
    offsets = [(1 + j) % n_rep for j in range(pairs)]
    remote = [j for j in range(pairs) if offsets[j]]

    barrier = pltpu.get_barrier_semaphore()
    for side in (up, down):
        pl.semaphore_signal(barrier, inc=1, device_id=(group, side), device_id_type=MESH)
    for j in remote:
        giver = lax.rem(group + offsets[j], n_rep)
        pl.semaphore_signal(barrier, inc=1, device_id=(giver, slab), device_id_type=MESH)
    pl.semaphore_wait(barrier, 2 + len(remote))

    def remote_copy(src, dst, send, recv, device):
        copy = pltpu.make_async_remote_copy(
            src_ref=src, dst_ref=dst, send_sem=send, recv_sem=recv, device_id=device, device_id_type=MESH
        )
        copy.start()
        return copy

    bond_copies = [remote_copy(coup.at[2, planes - width], low.at[2, 0], c_send.at[0], c_recv.at[0], (group, up))]
    if width > 1:
        bond_copies.append(
            remote_copy(coup.at[:, planes - width + 1 : planes], low.at[:, 1:width], c_send.at[1], c_recv.at[1], (group, up))
        )
        bond_copies.append(remote_copy(coup.at[:, 0 : width - 1], high, c_send.at[2], c_recv.at[2], (group, down)))

    row = lax.broadcasted_iota(jnp.int32, (half, cols), 0)
    site = row + lax.broadcasted_iota(jnp.int32, (half, cols), 1)

    def front(plane):
        return ((site + (slab * planes + plane + width)) & 1) == 0

    def pack(mask, first, second):
        second = reverse_rows(second, row)
        return jnp.where(mask, first, second), jnp.where(mask, second, first)

    copies = {}

    def send_halo(r, e):
        colour = (e * width) % 2
        below, above = halo_items(width, colour)
        for side, (items, start, device) in enumerate(((below, planes, up), (above, width, down))):
            for i, (d, c) in enumerate(items):
                for k in range(comps):
                    stage[e, side, r, i, k] = work[r, start + d, c, k]
            copies[r, e, side] = remote_copy(
                stage.at[e, side, r], land.at[e, side, r], h_send.at[e, side, r], h_recv.at[e, side, r], (group, device)
            )

    def take_halo(r, e):
        colour = (e * width) % 2
        below, above = halo_items(width, colour)
        for side, (items, start) in enumerate(((below, 0), (above, planes + width))):
            copies[r, e, side].wait()
            for i, (d, c) in enumerate(items):
                for k in range(comps):
                    work[r, start + d, c, k] = land[e, side, r, i, k]

    kept = []
    for slot in range(rep_dev):
        own = group * rep_dev + slot
        kept.append(source[own] == own)

    for r in range(pairs):

        def pack_plane(p, carry, r=r):
            mask = front(p + width)
            for k in range(comps):
                value = jnp.where(kept[2 * r], spins[2 * r, k, p], spins[2 * r + 1, k, p])
                zero, one = pack(mask, value[:half], value[half:])
                work[r, p + width, 0, k] = zero
                work[r, p + width, 1, k] = one
            return carry

        lax.fori_loop(0, planes, pack_plane, 0)
        send_halo(r, 0)

    def bonds_of(plane, jx, jy, jz, jz_below):
        mask = front(plane)
        jx, jy, jz, jz_below = [(2 * j - 1).astype(jnp.float32) for j in (jx, jy, jz, jz_below)]
        jw = pltpu.roll(jx, 1, 1)
        first, second = jy[:half], jy[half:]
        south_first = jnp.where(row == 0, second[half - 1 :], pltpu.roll(first, 1, 0))
        south_second = jnp.where(row == 0, first[half - 1 :], pltpu.roll(second, 1, 0))
        first_r = reverse_rows(second, row)
        south_r = reverse_rows(south_second, row)
        east = pack(mask, jx[:half], jx[half:])
        west = pack(mask, jw[:half], jw[half:])
        upper = pack(mask, jz[:half], jz[half:])
        lower = pack(mask, jz_below[:half], jz_below[half:])
        after = (jnp.where(mask, first, south_r), jnp.where(mask, south_r, first))
        before = (jnp.where(mask, south_first, first_r), jnp.where(mask, first_r, south_first))
        for i, bond in enumerate((east, west, after, before, upper, lower)):
            for c in range(2):
                bonds[plane, c, i] = bond[c]

    def own_bonds(p, carry):
        bonds_of(p + width, coup[0, p], coup[1, p], coup[2, p], coup[2, p - 1])
        return carry

    lax.fori_loop(1, planes, own_bonds, 0)
    for copy in bond_copies:
        copy.wait()
    for p in range(1, width):
        bonds_of(p, low[0, p], low[1, p], low[2, p], low[2, p - 1])
    bonds_of(width, coup[0, 0], coup[1, 0], coup[2, 0], low[2, width - 1])
    for p in range(width - 1):
        beneath = coup[2, planes - 1] if p == 0 else high[2, p - 1]
        bonds_of(planes + width + p, high[0, p], high[1, p], high[2, p], beneath)

    def half_sweep(r, colour, first, last):
        other = 1 - colour

        def one_plane(p, carry):
            east, west, after, before, upper, lower = [bonds[p, colour, i] for i in range(6)]
            field, spin = [], []
            for k in range(comps):
                q = work[r, p, other, k]
                north = jnp.where(row == half - 1, q, pltpu.roll(q, half - 1, 0))
                south = jnp.where(row == 0, q, pltpu.roll(q, 1, 0))
                h = east * pltpu.roll(q, cols - 1, 1) + west * pltpu.roll(q, 1, 1)
                h = h + after * north + before * south
                h = h + upper * work[r, p + 1, other, k] + lower * work[r, p - 1, other, k]
                field.append(h)
                spin.append(work[r, p, colour, k])
            along = sum(s * h for s, h in zip(spin, field))
            strength = sum(h * h for h in field)
            scale = 2.0 * along / jnp.maximum(strength, 1.0)
            for k in range(comps):
                work[r, p, colour, k] = scale * field[k] - spin[k]
            return carry

        lax.fori_loop(first, last, one_plane, 0)

    results = []
    for e in range(exchanges):
        for r in range(pairs):
            take_halo(r, e)
            for i in range(width):
                half_sweep(r, (e * width + i) % 2, i + 1, planes + 2 * width - 1 - i)
            if e < exchanges - 1:
                send_halo(r, e + 1)
            else:
                for n, j in enumerate(remote):
                    taker = lax.rem(group + n_rep - offsets[j], n_rep)
                    results.append(
                        remote_copy(
                            work.at[r, width : width + planes], res.at[n, r], r_send.at[n, r], r_recv.at[n, r], (taker, slab)
                        )
                    )

    def write(j):
        if j in remote:
            n = remote.index(j)
            given = lambda r, p, c, k: res[n, r, p, c, k]
        else:
            given = lambda r, p, c, k: work[r, p + width, c, k]

        def write_plane(p, carry):
            mask = front(p + width)
            for slot in (2 * j, 2 * j + 1):
                pair = lax.rem(source[group * rep_dev + slot], rep_dev) // 2
                for k in range(comps):
                    colours = []
                    for c in range(2):
                        value = given(0, p, c, k)
                        for r in range(1, pairs):
                            value = jnp.where(pair == r, given(r, p, c, k), value)
                        colours.append(jnp.where(kept[slot], work[j, p + width, c, k], value))
                    zero, one = colours
                    out[slot, k, p, :half] = jnp.where(mask, zero, one)
                    out[slot, k, p, half:] = reverse_rows(jnp.where(mask, one, zero), row)
            return carry

        lax.fori_loop(0, planes, write_plane, 0)

    for j in range(pairs):
        if j not in remote:
            write(j)
    for copy in results:
        copy.wait()
    for j in remote:
        write(j)


def solution(mesh):
    n_rep, n_slab = mesh.shape["rep"], mesh.shape["slab"]

    def local(spins, couplings, source):
        rep_dev, comps, planes, rows, cols = spins.shape
        pairs, half, width = rep_dev // 2, rows // 2, WIDTH
        exchanges, items = 2 * SWEEPS // width, 2 * width - 1
        n_remote = sum(1 for j in range(pairs) if (1 + j) % n_rep)
        deep = planes + 2 * width
        f32, i32, dma = jnp.float32, jnp.int32, pltpu.SemaphoreType.DMA
        return pl.pallas_call(
            functools.partial(kernel, n_rep, n_slab),
            out_shape=jax.ShapeDtypeStruct(spins.shape, f32),
            in_specs=[
                pl.BlockSpec(memory_space=pltpu.SMEM),
                pl.BlockSpec(memory_space=pltpu.VMEM),
                pl.BlockSpec(memory_space=pltpu.VMEM),
            ],
            out_specs=pl.BlockSpec(memory_space=pltpu.VMEM),
            scratch_shapes=[
                pltpu.VMEM((pairs, deep, 2, comps, half, cols), f32),
                pltpu.VMEM((deep, 2, 6, half, cols), f32),
                pltpu.VMEM((3, width, rows, cols), i32),
                pltpu.VMEM((3, max(width - 1, 1), rows, cols), i32),
                pltpu.VMEM((exchanges, 2, pairs, items, comps, half, cols), f32),
                pltpu.VMEM((exchanges, 2, pairs, items, comps, half, cols), f32),
                pltpu.VMEM((max(n_remote, 1), pairs, planes, 2, comps, half, cols), f32),
                dma((3,)),
                dma((3,)),
                dma((exchanges, 2, pairs)),
                dma((exchanges, 2, pairs)),
                dma((max(n_remote, 1), pairs)),
                dma((max(n_remote, 1), pairs)),
            ],
            compiler_params=pltpu.CompilerParams(collective_id=0, has_side_effects=True),
        )(source, spins, couplings)

    in_specs = (P("rep", None, "slab", None, None), P(None, "slab", None, None), P())
    out_specs = P("rep", None, "slab", None, None)
    return jax.shard_map(local, mesh=mesh, in_specs=in_specs, out_specs=out_specs, check_vma=False)
```

time: 130 us -> 51.3 us (0.39)
  waiting for transfers between devices: 71.8 us -> 0 us
  Pallas kernels: 0 us -> 48.5 us
  other arithmetic: 28.9 us -> 0 us
  local copies, waits for them, and re-layouts: 15.6 us -> 2.67 us
  starting transfers between devices: 12.2 us -> 0 us
    ppermute x19 -> x0, waiting for transfers between devices: 71.8 us -> none  [the longest x8 37.3 us: with_halo(): before = lax.ppermute(last, axis, up)]
    pallas_call x0 -> x1, Pallas kernels: none -> 48.5 us  [local(): pl.pallas_call(functools.partial(kernel, n_rep, n_slab), out_shape=jax.Sh...]
    reduce_sum x8 -> x0, other arithmetic: 16.2 us -> none  [relax(): along = jnp.sum(middle * local_field, axis=1, keepdims=True)]
    ppermute x19 -> x0, starting transfers between devices: 12.2 us -> none  [the longest x8 4.73 us: with_halo(): after = lax.ppermute(leading, axis, down)]
    slice x56 -> x0, local copies, waits for them, and re-layouts: 9.6 us -> none  [the longest x16 4.37 us: field(): east = bond_x * jnp.roll(middle, -1, axis=4)]
    mul x16 -> x0, other arithmetic: 7.25 us -> none  [the longest x8 5.79 us: field(): south = jnp.roll(bond_y * middle, 1, axis=3)]
    gather x5 -> x0, local copies, waits for them, and re-layouts: 4.64 us -> none  [the longest x2 2.72 us: outgoing(): return jnp.take(spins, asked % rep_dev, axis=0)]
    select_n x6 -> x0, other arithmetic: 3.71 us -> none  [the longest x2 2.1 us: outgoing(): return jnp.take(spins, asked % rep_dev, axis=0)]
  transfers between devices with their start and end apart: 19 -> 0, of which waited for: 17 -> 0; matrix products, arithmetic and copies ran while one was open for 9% -> 0% of each run, Pallas kernels for 0% -> 0%
where the time goes in v1:
time: 51.3 us; the launch traced here: 51.1 us
  Pallas kernels  48.5 us (95%)
  local copies, waits for them, and re-layouts  2.67 us (5%)
    pallas_call x1, Pallas kernels, local(): pl.pallas_call(functools.partial(kernel, n_rep, n_slab), out_shape=jax.Sh...  48.5 us
    unnamed x1, local copies, waits for them, and re-layouts  2.67 us

profile of v1, /device:TPU:0, one launch (start us, length us, event | category | flops | bytes accessed | tf_op | source)
XLA Modules:
  0.0 51.1 jit_solution(12797510114424172443)
XLA Ops:
  0.0 48.5 %shard_map.37 = f32[4,3,8,16,256]{4,3,2,1,0:T(8,128)} custom-call(s32[8]{0:T(128)} %source.1, f32[4,3,8,16,256]{4,3,2,1,0:T(8,128)} %spins.1, s32[3,8,16,256]{3,2,1,0:T(8,128)} %coup.1), custom_call_target="tpu_custom_call" | custom-call | tf_op jit(solution)/shard_map/pallas_call | solution.py:235
  48.5 2.7 %copy.5 = f32[4,3,8,16,256]{4,3,2,1,0:T(8,128)} copy(f32[4,3,8,16,256]{4,3,2,1,0:T(8,128)} %shard_map.37) | data formatting | bytes 3145728

commit v2 on v1

--- a/solution.py
+++ b/solution.py
@@ -8,6 +8,7 @@
 from jax.sharding import PartitionSpec as P
 
 SWEEPS = 4
+GROUP = 5
 WIDTH = 2
 MESH = pl.DeviceIdType.MESH
 
@@ -31,7 +32,7 @@
     return below, above
 
 
-def kernel(n_rep, n_slab, source, spins, coup, out, work, bonds, low, high, stage, land, res, c_send, c_recv, h_send, h_recv, r_send, r_recv):
+def kernel(n_rep, n_slab, source, spins_hbm, coup_hbm, out_hbm, spins, coup, out, raw, work, bonds, low, high, stage, land, res, c_send, c_recv, h_send, h_recv, r_send, r_recv, in_sem, out_sem):
     rep_dev, comps, planes, rows, cols = spins.shape
     pairs = rep_dev // 2
     width, half = WIDTH, rows // 2
@@ -41,27 +42,23 @@
     offsets = [(1 + j) % n_rep for j in range(pairs)]
     remote = [j for j in range(pairs) if offsets[j]]
 
+    loads = [pltpu.make_async_copy(spins_hbm.at[pl.ds(2 * r, 2)], spins.at[pl.ds(2 * r, 2)], in_sem.at[r]) for r in range(pairs)]
+    loads.append(pltpu.make_async_copy(coup_hbm, coup, in_sem.at[pairs]))
+    for copy in loads:
+        copy.start()
+
     barrier = pltpu.get_barrier_semaphore()
     for side in (up, down):
         pl.semaphore_signal(barrier, inc=1, device_id=(group, side), device_id_type=MESH)
     for j in remote:
         giver = lax.rem(group + offsets[j], n_rep)
         pl.semaphore_signal(barrier, inc=1, device_id=(giver, slab), device_id_type=MESH)
-    pl.semaphore_wait(barrier, 2 + len(remote))
-
     def remote_copy(src, dst, send, recv, device):
         copy = pltpu.make_async_remote_copy(
             src_ref=src, dst_ref=dst, send_sem=send, recv_sem=recv, device_id=device, device_id_type=MESH
         )
         copy.start()
         return copy
-
-    bond_copies = [remote_copy(coup.at[2, planes - width], low.at[2, 0], c_send.at[0], c_recv.at[0], (group, up))]
-    if width > 1:
-        bond_copies.append(
-            remote_copy(coup.at[:, planes - width + 1 : planes], low.at[:, 1:width], c_send.at[1], c_recv.at[1], (group, up))
-        )
-        bond_copies.append(remote_copy(coup.at[:, 0 : width - 1], high, c_send.at[2], c_recv.at[2], (group, down)))
 
     row = lax.broadcasted_iota(jnp.int32, (half, cols), 0)
     site = row + lax.broadcasted_iota(jnp.int32, (half, cols), 1)
@@ -101,6 +98,7 @@
         kept.append(source[own] == own)
 
     for r in range(pairs):
+        loads[r].wait()
 
         def pack_plane(p, carry, r=r):
             mask = front(p + width)
@@ -109,10 +107,12 @@
                 zero, one = pack(mask, value[:half], value[half:])
                 work[r, p + width, 0, k] = zero
                 work[r, p + width, 1, k] = one
+                if r == 0 and remote:
+                    raw[p, 0, k] = zero
+                    raw[p, 1, k] = one
             return carry
 
         lax.fori_loop(0, planes, pack_plane, 0)
-        send_halo(r, 0)
 
     def bonds_of(plane, jx, jy, jz, jz_below):
         mask = front(plane)
@@ -137,7 +137,23 @@
         bonds_of(p + width, coup[0, p], coup[1, p], coup[2, p], coup[2, p - 1])
         return carry
 
+    loads[pairs].wait()
     lax.fori_loop(1, planes, own_bonds, 0)
+    pl.semaphore_wait(barrier, 2 + len(remote))
+
+    bond_copies = [remote_copy(coup.at[2, planes - width], low.at[2, 0], c_send.at[0], c_recv.at[0], (group, up))]
+    if width > 1:
+        bond_copies.append(
+            remote_copy(coup.at[:, planes - width + 1 : planes], low.at[:, 1:width], c_send.at[1], c_recv.at[1], (group, up))
+        )
+        bond_copies.append(remote_copy(coup.at[:, 0 : width - 1], high, c_send.at[2], c_recv.at[2], (group, down)))
+    inner = pl.ds(width, planes)
+    results, late = [], []
+    for n, j in enumerate(remote):
+        taker = lax.rem(group + n_rep - offsets[j], n_rep)
+        late.append(remote_copy(raw, work.at[pairs + n, inner], r_send.at[n, 0], r_recv.at[n, 0], (taker, slab)))
+    for r in range(pairs - 1, -1, -1):
+        send_halo(r, 0)
     for copy in bond_copies:
         copy.wait()
     for p in range(1, width):
@@ -150,7 +166,7 @@
     def half_sweep(r, colour, first, last):
         other = 1 - colour
 
-        def one_plane(p, carry):
+        def turned(p):
             east, west, after, before, upper, lower = [bonds[p, colour, i] for i in range(6)]
             field, spin = [], []
             for k in range(comps):
@@ -165,33 +181,49 @@
             along = sum(s * h for s, h in zip(spin, field))
             strength = sum(h * h for h in field)
             scale = 2.0 * along / jnp.maximum(strength, 1.0)
-            for k in range(comps):
-                work[r, p, colour, k] = scale * field[k] - spin[k]
+            return [scale * h - s for s, h in zip(spin, field)]
+
+        count = last - first
+        step = max(g for g in range(1, GROUP + 1) if count % g == 0)
+
+        def some_planes(i, carry):
+            base = first + i * step
+            new = [turned(base + n) for n in range(step)]
+            for n in range(step):
+                for k in range(comps):
+                    work[r, base + n, colour, k] = new[n][k]
             return carry
 
-        lax.fori_loop(first, last, one_plane, 0)
-
-    results = []
+        lax.fori_loop(0, count // step, some_planes, 0)
+
+    def advance(r, e):
+        take_halo(r, e)
+        for i in range(width):
+            half_sweep(r, (e * width + i) % 2, i + 1, planes + 2 * width - 1 - i)
+        if e < exchanges - 1:
+            send_halo(r, e + 1)
+        elif 1 <= r < pairs:
+            for n, j in enumerate(remote):
+                taker = lax.rem(group + n_rep - offsets[j], n_rep)
+                results.append(
+                    remote_copy(work.at[r, inner], res.at[n, r - 1], r_send.at[n, r], r_recv.at[n, r], (taker, slab))
+                )
+
     for e in range(exchanges):
-        for r in range(pairs):
-            take_halo(r, e)
-            for i in range(width):
-                half_sweep(r, (e * width + i) % 2, i + 1, planes + 2 * width - 1 - i)
-            if e < exchanges - 1:
-                send_halo(r, e + 1)
-            else:
-                for n, j in enumerate(remote):
-                    taker = lax.rem(group + n_rep - offsets[j], n_rep)
-                    results.append(
-                        remote_copy(
-                            work.at[r, width : width + planes], res.at[n, r], r_send.at[n, r], r_recv.at[n, r], (taker, slab)
-                        )
-                    )
+        for r in range(pairs - 1, -1, -1):
+            advance(r, e)
+        if e == 0:
+            for n, copy in enumerate(late):
+                copy.wait_recv()
+                send_halo(pairs + n, 0)
+        elif e < exchanges - 1:
+            for n in range(len(late)):
+                advance(pairs + n, e - 1)
 
     def write(j):
         if j in remote:
             n = remote.index(j)
-            given = lambda r, p, c, k: res[n, r, p, c, k]
+            given = lambda r, p, c, k: res[n, r - 1, p, c, k] if r else work[pairs + n, p + width, c, k]
         else:
             given = lambda r, p, c, k: work[r, p + width, c, k]
 
@@ -213,13 +245,27 @@
 
         lax.fori_loop(0, planes, write_plane, 0)
 
+    stores = []
+
+    def store(j):
+        write(j)
+        stores.append(pltpu.make_async_copy(out.at[pl.ds(2 * j, 2)], out_hbm.at[pl.ds(2 * j, 2)], out_sem.at[j]))
+        stores[-1].start()
+
     for j in range(pairs):
         if j not in remote:
-            write(j)
+            store(j)
+    for e in range(max(exchanges - 2, 0), exchanges):
+        for n in range(len(late)):
+            advance(pairs + n, e)
+    for copy in late:
+        copy.wait_send()
     for copy in results:
         copy.wait()
     for j in remote:
-        write(j)
+        store(j)
+    for copy in stores:
+        copy.wait()
 
 
 def solution(mesh):
@@ -237,24 +283,30 @@
             out_shape=jax.ShapeDtypeStruct(spins.shape, f32),
             in_specs=[
                 pl.BlockSpec(memory_space=pltpu.SMEM),
-                pl.BlockSpec(memory_space=pltpu.VMEM),
-                pl.BlockSpec(memory_space=pltpu.VMEM),
+                pl.BlockSpec(memory_space=pl.ANY),
+                pl.BlockSpec(memory_space=pl.ANY),
             ],
-            out_specs=pl.BlockSpec(memory_space=pltpu.VMEM),
+            out_specs=pl.BlockSpec(memory_space=pl.ANY),
             scratch_shapes=[
-                pltpu.VMEM((pairs, deep, 2, comps, half, cols), f32),
+                pltpu.VMEM(spins.shape, f32),
+                pltpu.VMEM(couplings.shape, i32),
+                pltpu.VMEM(spins.shape, f32),
+                pltpu.VMEM((planes, 2, comps, half, cols), f32),
+                pltpu.VMEM((pairs + n_remote, deep, 2, comps, half, cols), f32),
                 pltpu.VMEM((deep, 2, 6, half, cols), f32),
                 pltpu.VMEM((3, width, rows, cols), i32),
                 pltpu.VMEM((3, max(width - 1, 1), rows, cols), i32),
-                pltpu.VMEM((exchanges, 2, pairs, items, comps, half, cols), f32),
-                pltpu.VMEM((exchanges, 2, pairs, items, comps, half, cols), f32),
-                pltpu.VMEM((max(n_remote, 1), pairs, planes, 2, comps, half, cols), f32),
+                pltpu.VMEM((exchanges, 2, pairs + n_remote, items, comps, half, cols), f32),
+                pltpu.VMEM((exchanges, 2, pairs + n_remote, items, comps, half, cols), f32),
+                pltpu.VMEM((max(n_remote, 1), pairs - 1, planes, 2, comps, half, cols), f32),
                 dma((3,)),
                 dma((3,)),
-                dma((exchanges, 2, pairs)),
-                dma((exchanges, 2, pairs)),
+                dma((exchanges, 2, pairs + n_remote)),
+                dma((exchanges, 2, pairs + n_remote)),
                 dma((max(n_remote, 1), pairs)),
                 dma((max(n_remote, 1), pairs)),
+                dma((pairs + 1,)),
+                dma((pairs,)),
             ],
             compiler_params=pltpu.CompilerParams(collective_id=0, has_side_effects=True),
         )(source, spins, couplings)

time: 51.3 us -> 40.3 us (0.79)
  Pallas kernels: 48.5 us -> 37.5 us
    pallas_call x1, Pallas kernels: 48.5 us -> 37.5 us  [local(): pl.pallas_call(functools.partial(kernel, n_rep, n_slab), out_shape=jax.Sh...]
where the time goes in v2:
time: 40.3 us; the launch traced here: 40.2 us
  Pallas kernels  37.5 us (93%)
  local copies, waits for them, and re-layouts  2.67 us (7%)
    pallas_call x1, Pallas kernels, local(): pl.pallas_call(functools.partial(kernel, n_rep, n_slab), out_shape=jax.Sh...  37.5 us
    unnamed x1, local copies, waits for them, and re-layouts  2.67 us

profile of v2, /device:TPU:0, one launch (start us, length us, event | category | flops | bytes accessed | tf_op | source)
XLA Modules:
  0.0 40.2 jit_solution(470148052807253794)
XLA Ops:
  0.0 37.5 %shard_map.37 = f32[4,3,8,16,256]{4,3,2,1,0:T(8,128)} custom-call(s32[8]{0:T(128)} %source.1, f32[4,3,8,16,256]{4,3,2,1,0:T(8,128)} %spins_hbm.1, s32[3,8,16,256]{3,2,1,0:T(8,128)} %coup_hbm.1), custom_call_target="tpu_custom_call" | custom-call | tf_op jit(solution)/shard_map/pallas_call | solution.py:281
  37.5 2.7 %copy.5 = f32[4,3,8,16,256]{4,3,2,1,0:T(8,128)} copy(f32[4,3,8,16,256]{4,3,2,1,0:T(8,128)} %shard_map.37) | data formatting | bytes 3145728

commit v3 on v2

--- a/solution.py
+++ b/solution.py
@@ -26,9 +26,12 @@
     return value
 
 
-def halo_items(width, colour):
+def halo_items(width, colour, first):
     below = [(0, 1 - colour)] + [(d, c) for d in range(1, width) for c in range(2)]
     above = [(d, c) for d in range(width - 1) for c in range(2)] + [(width - 1, 1 - colour)]
+    if not first and width % 2 == 0:
+        below.remove((width - 1, 0))
+        above.remove((0, 0))
     return below, above
 
 
@@ -74,18 +77,21 @@
 
     def send_halo(r, e):
         colour = (e * width) % 2
-        below, above = halo_items(width, colour)
+        below, above = halo_items(width, colour, e == 0)
         for side, (items, start, device) in enumerate(((below, planes, up), (above, width, down))):
             for i, (d, c) in enumerate(items):
                 for k in range(comps):
                     stage[e, side, r, i, k] = work[r, start + d, c, k]
             copies[r, e, side] = remote_copy(
-                stage.at[e, side, r], land.at[e, side, r], h_send.at[e, side, r], h_recv.at[e, side, r], (group, device)
+                stage.at[e, side, r, pl.ds(0, len(items))],
+                land.at[e, side, r, pl.ds(0, len(items))], h_send.at[e, side, r],
+                h_recv.at[e, side, r],
+                (group, device),
             )
 
     def take_halo(r, e):
         colour = (e * width) % 2
-        below, above = halo_items(width, colour)
+        below, above = halo_items(width, colour, e == 0)
         for side, (items, start) in enumerate(((below, 0), (above, planes + width))):
             copies[r, e, side].wait()
             for i, (d, c) in enumerate(items):

time: 40.3 us -> 38.3 us (0.950)
  Pallas kernels: 37.5 us -> 35.4 us
    pallas_call x1, Pallas kernels: 37.5 us -> 35.4 us  [local(): pl.pallas_call(functools.partial(kernel, n_rep, n_slab), out_shape=jax.Sh...]
where the time goes in v3:
time: 38.3 us; the launch traced here: 38.1 us
  Pallas kernels  35.4 us (92%)
  local copies, waits for them, and re-layouts  2.67 us (7%)
    pallas_call x1, Pallas kernels, local(): pl.pallas_call(functools.partial(kernel, n_rep, n_slab), out_shape=jax.Sh...  35.4 us
    unnamed x1, local copies, waits for them, and re-layouts  2.67 us

profile of v3, /device:TPU:0, one launch (start us, length us, event | category | flops | bytes accessed | tf_op | source)
XLA Modules:
  0.0 38.1 jit_solution(4070340295064229700)
XLA Ops:
  0.0 35.4 %shard_map.37 = f32[4,3,8,16,256]{4,3,2,1,0:T(8,128)} custom-call(s32[8]{0:T(128)} %source.1, f32[4,3,8,16,256]{4,3,2,1,0:T(8,128)} %spins_hbm.1, s32[3,8,16,256]{3,2,1,0:T(8,128)} %coup_hbm.1), custom_call_target="tpu_custom_call" | custom-call | tf_op jit(solution)/shard_map/pallas_call | solution.py:287
  35.4 2.7 %copy.5 = f32[4,3,8,16,256]{4,3,2,1,0:T(8,128)} copy(f32[4,3,8,16,256]{4,3,2,1,0:T(8,128)} %shard_map.37) | data formatting | bytes 3145728
